TPU v7x, 32 devices: a whole 2x2x4 slice. The times are simulated.
32 devices in a mesh: gx: 8 (over y, x, core), yz: 4 (over z).
Axes of the slice: x: 2, y: 2, z: 4, core: 2. Of those that a mesh axis runs over, the one named last changes fastest.
Arguments:
- residual: float32 [96, 8, 64, 128], P('gx', 'yz'), may hold values from -0.3 to 0.3
- inverses: float32 [96, 8, 64, 64], P('gx', 'yz'), may hold values from -0.25 to 1
- upwind: float32 [8, 64, 64], replicated, may hold values from -0.25 to 1
- downwind: float32 [8, 64, 64], replicated, may hold values from -0.25 to 1
- flux_y: float32 [8, 64, 64], replicated, may hold values from -0.75 to 0.75
- kinds: int32 [8], P('yz'), may hold values from 0 to 7
- volume_category: int32 [96, 8, 128], P('gx', 'yz'), may hold values from 0 to 2, as said below
Outputs:
- adjoint: float32 [96, 8, 64, 128], P('gx', 'yz')
Inputs may be any that keep to these rules, and one draw needn't show every extreme that they name: `volume_category`: 0 marks a fluid cell, 1 a wall cell, 2 an inflow cell.
All inputs are finite; a program needn't handle non-finite values.
Results may differ from a plain program's by a relative error of at most 0.00026.
Values sent between devices are 32-bit elements; how exact they have to be, the bound alone decides.
A program may use at most 64 MiB of HBM per device.

v0:
```python
import functools

import jax
import jax.numpy as jnp
from jax import lax
from jax.experimental import pallas as pl
from jax.experimental.pallas import tpu as pltpu
from jax.sharding import PartitionSpec as P

MESH = pl.DeviceIdType.MESH
F32 = jnp.float32
BF16 = jnp.bfloat16


def split(a):
    high = a.astype(BF16)
    return high, (a - high.astype(F32)).astype(BF16)


def mul(a, b):
    ah, al = a
    bh, bl = b
    d = functools.partial(jnp.dot, preferred_element_type=F32)
    return d(ah, bh) + (d(ah, bl) + d(al, bh))


def loop(count, body, carry, unroll=1):
    unroll = unroll if count % unroll == 0 else 1

    def several(i, carry):
        for u in range(unroll):
            carry = body(i * unroll + u, carry)
        return carry

    return lax.fori_loop(0, count // unroll, several, carry)


def kernel(
    n_gx, n_yz, chunk, res_hbm, inv_hbm, up_hbm, down_hbm, flux_hbm, cat_hbm, kinds_hbm, out,
    res, inv, up, down, flux, cat, kinds,
    snd, low, high, table, vt, ft, bt, hom, omega, lam, resp, cs, gmap, gvec, wc, wl, into, side, wide_state, tall, into_state,
    load_sem, halo_send, halo_recv, map_send, map_recv, vec_send, vec_recv,
):
    cells, groups, nv, nz = res.shape
    half = n_gx // 2
    pieces = cells // chunk
    gx = lax.axis_index("gx")
    yz = lax.axis_index("yz")
    partner = gx + 1 - 2 * lax.rem(gx, 2)
    has_low = yz > 0
    has_high = yz < n_yz - 1

    loads = [
        pltpu.make_async_copy(source, target, load_sem.at[n])
        for n, (source, target) in enumerate(
            (
                (res_hbm, res), (inv_hbm, inv), (up_hbm, up), (down_hbm, down),
                (flux_hbm, flux), (cat_hbm, cat), (kinds_hbm, kinds),
            )
        )
    ]
    for load in loads:
        load.start()

    def peer(k):
        return lax.rem(gx + 2 * k, n_gx)

    barrier = pltpu.get_barrier_semaphore()
    for k in range(1, half):
        pl.semaphore_signal(barrier, inc=1, device_id=(peer(k), yz), device_id_type=MESH)
    pl.semaphore_signal(barrier, inc=1, device_id=(partner, yz), device_id_type=MESH)

    @pl.when(has_low)
    def _():
        pl.semaphore_signal(barrier, inc=1, device_id=(gx, yz - 1), device_id_type=MESH)

    @pl.when(has_high)
    def _():
        pl.semaphore_signal(barrier, inc=1, device_id=(gx, yz + 1), device_id_type=MESH)

    pl.semaphore_wait(barrier, half + jnp.where(has_low, 1, 0) + jnp.where(has_high, 1, 0))

    def halo(direction, g, c):
        part = pl.ds(c * chunk, chunk)
        if direction == 0:
            src = snd.at[0, part] if g == 0 else res_hbm.at[part, 1]
            dst, where = low, yz + 1
        else:
            src = res_hbm.at[part, 0] if g == 0 else snd.at[1, part]
            dst, where = high, yz - 1
        return pltpu.make_async_remote_copy(
            src_ref=src,
            dst_ref=dst.at[g, part],
            send_sem=halo_send.at[direction, g, c],
            recv_sem=halo_recv.at[direction, g, c],
            device_id=(gx, where),
            device_id_type=MESH,
        )

    @pl.when(has_low)
    def _():
        for c in range(pieces):
            halo(1, 0, c).start()

    loads[0].wait()

    for c in range(pieces):
        for x in range(c * chunk, (c + 1) * chunk):
            snd[0, x] = res[x, 0] - 8.0 * res[x, 1]

        @pl.when(has_high)
        def _():
            halo(0, 0, c).start()

    @pl.when(has_high)
    def _():
        for c in range(pieces):
            halo(0, 1, c).start()

    for c in range(pieces):
        for x in range(c * chunk, (c + 1) * chunk):
            snd[1, x] = 8.0 * res[x, 0] - res[x, 1]

        @pl.when(has_low)
        def _():
            halo(1, 1, c).start()

    @pl.when(jnp.logical_not(has_low))
    def _():
        low[...] = jnp.zeros_like(low)

    @pl.when(jnp.logical_not(has_high))
    def _():
        high[...] = jnp.zeros_like(high)

    for load in loads[1:]:
        load.wait()

    for g in range(groups):
        kind = kinds[g]
        for n, block in enumerate((flux[kind] * (1.0 / 12.0), -up[kind], -down[kind])):
            table[g, n, 0], table[g, n, 1] = split(block.T)

    def held(g, n):
        return table[g, n, 0], table[g, n, 1]

    def put(ref, g, x, pair):
        ref[g, x, 0], ref[g, x, 1] = pair

    def get(ref, g, x):
        return ref[g, x, 0], ref[g, x, 1]

    def steps(x, carry):
        for g in range(groups):
            v = split(inv[x, g].T)
            put(vt, g, x, v)
            put(ft, g, x, split(mul(v, held(g, 1))))
            put(bt, g, x, split(mul(v, held(g, 2))))
        return carry

    loop(cells, steps, 0, 4)

    row = lax.broadcasted_iota(jnp.int32, (nv, 2 * nv), 0)
    col = lax.broadcasted_iota(jnp.int32, (nv, 2 * nv), 1)
    first_unit = (row == col).astype(F32)
    second_unit = (row + nv == col).astype(F32)
    square_row = lax.broadcasted_iota(jnp.int32, (nv, nv), 0)
    square_col = lax.broadcasted_iota(jnp.int32, (nv, nv), 1)
    unit = (square_row == square_col).astype(F32)
    for g in range(groups):
        hom[g, 0] = first_unit
        omega[g, 0] = unit

    def hom_forward(x, carry):
        for g in range(groups):
            hom[g, x + 1] = mul(get(ft, g, x), split(hom[g, x]))
            omega[g, x + 1] = mul(split(omega[g, x]), get(bt, g, x))
        return carry

    loop(cells, hom_forward, 0)

    for g in range(groups):
        side[g] = jnp.zeros((nv, nv), F32)
        wide_state[g] = second_unit

    def hom_backward(i, carry):
        x = cells - 1 - i
        for g in range(groups):
            m = hom[g, x + 1] + mul(get(bt, g, x), split(wide_state[g]))
            put(resp, g, x, split(m))
            wide_state[g] = m
            now = split(omega[g, x] + side[g])
            put(lam, g, x, now)
            side[g] = mul(now, get(ft, g, x))
        return carry

    loop(cells, hom_backward, 0)
    for g in range(groups):
        gmap[gx, g * nv : (g + 1) * nv] = wide_state[g]
    gmap[gx, groups * nv :] = jnp.concatenate(
        [hom[g, cells][:, :nv] for g in range(groups)], axis=1
    )

    def share(buffer, send, recv, slot, target, k):
        return pltpu.make_async_remote_copy(
            src_ref=buffer.at[slot],
            dst_ref=buffer.at[slot],
            send_sem=send.at[k],
            recv_sem=recv.at[slot],
            device_id=(target, yz),
            device_id_type=MESH,
        )

    def offer(*where):
        for k in range(1, half):
            share(*where, gx, peer(k), k).start()
        share(*where, gx, partner, 0).start()

    def relay(*where):
        for k in range(1, half):
            share(*where, peer(k), peer(k), k).wait_recv()
            share(*where, peer(k), partner, half + k).start()

    def collect(*where):
        share(*where, partner, partner, 0).wait_recv()
        for k in range(1, half):
            share(*where, lax.rem(partner + 2 * k, n_gx), partner, half + k).wait_recv()

    def release(*where):
        share(*where, gx, partner, 0).wait_send()
        for k in range(1, half):
            share(*where, gx, peer(k), k).wait_send()
            share(*where, peer(k), partner, half + k).wait_send()

    maps = (gmap, map_send, map_recv)
    vecs = [(gvec.at[g], vec_send.at[g], vec_recv.at[g]) for g in range(groups)]
    offer(*maps)

    def local_forward(g):
        state = (jnp.zeros((nv, nz), F32), jnp.zeros((nv, nz), F32))
        for c in range(pieces):
            @pl.when(has_low)
            def _():
                halo(0, g, c).wait_recv()

            @pl.when(has_high)
            def _():
                halo(1, g, c).wait_recv()

            def forward(i, state):
                x = c * chunk + i
                last, first = state
                if g == 0:
                    derivative = 8.0 * res[x, 1] + low[g, x] - high[g, x]
                else:
                    derivative = low[g, x] + high[g, x] - 8.0 * res[x, 0]
                kind = cat[x][g : g + 1]
                weight = jnp.where(kind == 0, 1.0, jnp.where(kind == 2, 0.5, 0.0))
                force = weight * (res[x, g] + mul(held(g, 0), split(derivative)))
                driven = mul(get(vt, g, x), split(force))
                last = driven + mul(get(ft, g, x), split(last))
                first = first + mul(get(lam, g, x), split(driven))
                cs[g, x] = last
                return last, first

            state = loop(chunk, forward, state, chunk)
        gvec[g, gx, :nv] = state[0]
        gvec[g, gx, nv:] = state[1]

    def local_backward():
        for g in range(groups):
            into_state[g] = cs[g, cells - 1]

        def backward(i, carry):
            x = cells - 2 - i
            for g in range(groups):
                state = cs[g, x] + mul(get(bt, g, x), split(into_state[g]))
                into_state[g] = state
                cs[g, x] = state
            return carry

        lax.fori_loop(0, cells - 1, backward, 0)

    def finish(g):
        total = jnp.zeros((2 * nv, nz), F32)
        tail = jnp.zeros((nv, nz), F32)
        for j in range(n_gx):
            total = total + mul(get(wc, g, j), split(gvec[g, j, :nv]))
            tail = tail + mul(get(wl, g, j), split(gvec[g, j, nv:]))
        into[g, 0, :nv], into[g, 1, :nv] = split(total[:nv])
        into[g, 0, nv:], into[g, 1, nv:] = split(total[nv:] + tail)

        def fix(x, carry):
            value = cs[g, x] + mul(get(resp, g, x), (into[g, 0], into[g, 1]))
            out[x, g] = jnp.where(cat[x][g : g + 1] != 1, value, 0.0)
            return carry

        loop(cells, fix, 0, 4)

    local_forward(0)
    offer(*vecs[0])
    relay(*maps)
    collect(*maps)

    for g in range(groups):
        side[g] = jnp.zeros((nv, nv), F32)
        tall[g] = jnp.zeros((2 * nv, nv), F32)

    def suffix(j, carry):
        here = jnp.where(gx == j, 1.0, 0.0)
        for g in range(groups):
            e = split(side[g])
            put(wl, g, j, e)
            both = mul(e, split(gmap[j, g * nv : (g + 1) * nv]))
            side[g] = both[:, nv:] + here * unit
            hom[g, j] = both
        return carry

    loop(n_gx, suffix, 0)

    def prefix(i, carry):
        j = n_gx - 1 - i
        here = jnp.where(gx == j, 1.0, 0.0)
        maps_here = gmap[j, groups * nv :]
        for g in range(groups):
            xs = split(tall[g])
            put(wc, g, j, xs)
            nxt = mul(xs, split(maps_here[:, g * nv : (g + 1) * nv]))
            tall[g, :nv] = nxt[:nv] + here * unit
            tall[g, nv:] = nxt[nv:] + hom[g, j][:, :nv]
        return carry

    loop(n_gx, prefix, 0)

    relay(*vecs[0])
    for g in range(1, groups):
        local_forward(g)
        offer(*vecs[g])
    local_backward()
    for g in range(1, groups):
        relay(*vecs[g])
    for g in range(groups):
        collect(*vecs[g])
        finish(g)

    @pl.when(has_high)
    def _():
        for g in range(groups):
            for c in range(pieces):
                halo(0, g, c).wait_send()

    @pl.when(has_low)
    def _():
        for g in range(groups):
            for c in range(pieces):
                halo(1, g, c).wait_send()

    release(*maps)
    for g in range(groups):
        release(*vecs[g])


def per_device(n_gx, n_yz, residual, inverses, upwind, downwind, flux_y, kinds, volume_category):
    cells, groups, nv, nz = residual.shape
    chunk = next(c for c in (3, 4, 2, 1) if cells % c == 0)
    pieces = cells // chunk
    hbm = pl.BlockSpec(memory_space=pltpu.HBM)
    operands = (residual, inverses, upwind, downwind, flux_y, volume_category, kinds)
    square = pltpu.VMEM((groups, cells, 2, nv, nv), BF16)
    wide = pltpu.VMEM((groups, cells, nv, nz), F32)
    return pl.pallas_call(
        functools.partial(kernel, n_gx, n_yz, chunk),
        out_shape=jax.ShapeDtypeStruct(residual.shape, F32),
        in_specs=[hbm] * 7,
        out_specs=pl.BlockSpec(memory_space=pltpu.VMEM),
        scratch_shapes=[pltpu.VMEM(a.shape, a.dtype) for a in operands[:-1]]
        + [
            pltpu.SMEM(kinds.shape, kinds.dtype),
            pltpu.VMEM((2, cells, nv, nz), F32),
            wide,
            wide,
            pltpu.VMEM((groups, 3, 2, nv, nv), BF16),
            square,
            square,
            square,
            pltpu.VMEM((groups, max(cells, n_gx) + 1, nv, 2 * nv), F32),
            pltpu.VMEM((groups, cells + 1, nv, nv), F32),
            square,
            pltpu.VMEM((groups, cells, 2, nv, 2 * nv), BF16),
            wide,
            pltpu.VMEM((n_gx, (groups + 1) * nv, 2 * nv), F32),
            pltpu.VMEM((groups, n_gx, 2 * nv, nz), F32),
            pltpu.VMEM((groups, n_gx, 2, 2 * nv, nv), BF16),
            pltpu.VMEM((groups, n_gx, 2, nv, nv), BF16),
            pltpu.VMEM((groups, 2, 2 * nv, nz), BF16),
            pltpu.VMEM((groups, nv, nv), F32),
            pltpu.VMEM((groups, nv, 2 * nv), F32),
            pltpu.VMEM((groups, 2 * nv, nv), F32),
            pltpu.VMEM((groups, nv, nz), F32),
            pltpu.SemaphoreType.DMA((7,)),
            pltpu.SemaphoreType.DMA((2, groups, pieces)),
            pltpu.SemaphoreType.DMA((2, groups, pieces)),
            pltpu.SemaphoreType.DMA((n_gx,)),
            pltpu.SemaphoreType.DMA((n_gx,)),
            pltpu.SemaphoreType.DMA((groups, n_gx)),
            pltpu.SemaphoreType.DMA((groups, n_gx)),
        ],
        compiler_params=pltpu.CompilerParams(
            collective_id=0, has_side_effects=True, vmem_limit_bytes=48 * 1024 * 1024
        ),
    )(*(pltpu.with_memory_space_constraint(a, pltpu.HBM) for a in operands))


def solution(mesh):
    in_specs = (
        P("gx", "yz", None, None),
        P("gx", "yz", None, None),
        P(),
        P(),
        P(),
        P("yz"),
        P("gx", "yz", None),
    )
    out_specs = P("gx", "yz", None, None)
    return jax.shard_map(
        functools.partial(per_device, mesh.shape["gx"], mesh.shape["yz"]),
        mesh=mesh,
        in_specs=in_specs,
        out_specs=out_specs,
        check_vma=False,
    )
```

profile of v0, /device:TPU:0, one launch (start us, length us, event | category | flops | bytes accessed | tf_op | source)
XLA Modules:
  0.0 32.6 jit_solution(17313577669191444048)
XLA Ops:
  0.0 31.7 %shard_map.73 = f32[12,2,64,128]{3,2,1,0:T(8,128)S(1)} custom-call(f32[12,2,64,128]{3,2,1,0:T(8,128)} %res_hbm.1, f32[12,2,64,64]{3,2,1,0:T(8,128)} %inv_hbm.1, f32[8,64,64]{2,1,0:T(8,128)} %up_hbm.1, f32[8,64,64]{2,1,0:T(8,128)} %down_hbm.1, f32[8,64,64]{2,1,0:T(8,128)} %flux_hbm.1, s32[12,2,128]{2,1,0:T(2,128)} %cat_hbm.1, s32[2]{0:T(128)} %kinds_hbm.1), custom_call_target="tpu_custom_call" | custom-call | tf_op jit(solution)/shard_map/pallas_call | solution.py:371
  31.7 0.9 %copy.9 = f32[12,2,64,128]{3,2,1,0:T(8,128)} copy(f32[12,2,64,128]{3,2,1,0:T(8,128)S(1)} %shard_map.73) | data formatting | bytes 1572864
where the time goes:
time: 32.7 us; the launch traced here: 32.6 us
  Pallas kernels  31.7 us (97%)
  local copies, waits for them, and re-layouts  0.88 us (3%)
    pallas_call x1, Pallas kernels, per_device(): pl.pallas_call(functools.partial(kernel, n_gx, n_yz, chunk), out_shape=ja...  31.7 us
    unnamed x1, local copies, waits for them, and re-layouts  0.88 us

commit v1 on v0

--- a/solution.py
+++ b/solution.py
@@ -38,7 +38,8 @@
 def kernel(
     n_gx, n_yz, chunk, res_hbm, inv_hbm, up_hbm, down_hbm, flux_hbm, cat_hbm, kinds_hbm, out,
     res, inv, up, down, flux, cat, kinds,
-    snd, low, high, table, vt, ft, bt, hom, omega, lam, resp, cs, gmap, gvec, wc, wl, into, side, wide_state, tall, into_state,
+    snd, low, high, table, vt, ft, bt, hom, omega, gain, fast, resp, cs, acc, gmap, given, taken,
+    send_map, ahead, behind, mirror, wide_state, tall, into_state,
     load_sem, halo_send, halo_recv, map_send, map_recv, vec_send, vec_recv,
 ):
     cells, groups, nv, nz = res.shape
@@ -66,9 +67,10 @@
         return lax.rem(gx + 2 * k, n_gx)
 
     barrier = pltpu.get_barrier_semaphore()
-    for k in range(1, half):
-        pl.semaphore_signal(barrier, inc=1, device_id=(peer(k), yz), device_id_type=MESH)
-    pl.semaphore_signal(barrier, inc=1, device_id=(partner, yz), device_id_type=MESH)
+    for k in range(1, n_gx):
+        pl.semaphore_signal(
+            barrier, inc=1, device_id=(lax.rem(gx + k, n_gx), yz), device_id_type=MESH
+        )
 
     @pl.when(has_low)
     def _():
@@ -78,7 +80,7 @@
     def _():
         pl.semaphore_signal(barrier, inc=1, device_id=(gx, yz + 1), device_id_type=MESH)
 
-    pl.semaphore_wait(barrier, half + jnp.where(has_low, 1, 0) + jnp.where(has_high, 1, 0))
+    pl.semaphore_wait(barrier, n_gx - 1 + jnp.where(has_low, 1, 0) + jnp.where(has_high, 1, 0))
 
     def halo(direction, g, c):
         part = pl.ds(c * chunk, chunk)
@@ -180,18 +182,21 @@
     loop(cells, hom_forward, 0)
 
     for g in range(groups):
-        side[g] = jnp.zeros((nv, nv), F32)
+        tall[g, :nv] = unit
+        tall[g, nv:] = jnp.zeros((nv, nv), F32)
         wide_state[g] = second_unit
 
     def hom_backward(i, carry):
         x = cells - 1 - i
         for g in range(groups):
             m = hom[g, x + 1] + mul(get(bt, g, x), split(wide_state[g]))
-            put(resp, g, x, split(m))
+            resp[g, 0, x], resp[g, 1, x] = split(m)
             wide_state[g] = m
-            now = split(omega[g, x] + side[g])
-            put(lam, g, x, now)
-            side[g] = mul(now, get(ft, g, x))
+            now = split(
+                jnp.concatenate([tall[g, :nv], omega[g, x] + tall[g, nv:]], axis=0)
+            )
+            put(gain, g, x, split(mul(now, get(vt, g, x))))
+            tall[g] = mul(now, get(ft, g, x))
         return carry
 
     loop(cells, hom_backward, 0)
@@ -233,114 +238,186 @@
             share(*where, peer(k), partner, half + k).wait_send()
 
     maps = (gmap, map_send, map_recv)
-    vecs = [(gvec.at[g], vec_send.at[g], vec_recv.at[g]) for g in range(groups)]
     offer(*maps)
 
-    def local_forward(g):
-        state = (jnp.zeros((nv, nz), F32), jnp.zeros((nv, nz), F32))
-        for c in range(pieces):
-            @pl.when(has_low)
-            def _():
-                halo(0, g, c).wait_recv()
-
-            @pl.when(has_high)
-            def _():
-                halo(1, g, c).wait_recv()
-
-            def forward(i, state):
-                x = c * chunk + i
-                last, first = state
-                if g == 0:
-                    derivative = 8.0 * res[x, 1] + low[g, x] - high[g, x]
-                else:
-                    derivative = low[g, x] + high[g, x] - 8.0 * res[x, 0]
-                kind = cat[x][g : g + 1]
-                weight = jnp.where(kind == 0, 1.0, jnp.where(kind == 2, 0.5, 0.0))
-                force = weight * (res[x, g] + mul(held(g, 0), split(derivative)))
-                driven = mul(get(vt, g, x), split(force))
-                last = driven + mul(get(ft, g, x), split(last))
-                first = first + mul(get(lam, g, x), split(driven))
-                cs[g, x] = last
-                return last, first
-
-            state = loop(chunk, forward, state, chunk)
-        gvec[g, gx, :nv] = state[0]
-        gvec[g, gx, nv:] = state[1]
-
-    def local_backward():
-        for g in range(groups):
-            into_state[g] = cs[g, cells - 1]
+    edge = cells - chunk
+
+    def weight(g, x):
+        kind = cat[x][g : g + 1]
+        return jnp.where(kind == 0, 1.0, jnp.where(kind == 2, 0.5, 0.0))
+
+    def slope(g, x):
+        if g == 0:
+            return 8.0 * res[x, 1] + low[g, x] - high[g, x]
+        return low[g, x] + high[g, x] - 8.0 * res[x, 0]
+
+    def arrive(g, c):
+        @pl.when(has_low)
+        def _():
+            halo(0, g, c).wait_recv()
+
+        @pl.when(has_high)
+        def _():
+            halo(1, g, c).wait_recv()
+
+    def local_forward(g, c, state, gather):
+        for x in range(c * chunk, (c + 1) * chunk):
+            force = split(weight(g, x) * (res[x, g] + mul(held(g, 0), split(slope(g, x)))))
+            driven = mul(get(vt, g, x), force)
+            state = driven + mul(get(ft, g, x), split(state))
+            cs[g, x] = state
+            if gather:
+                acc[g] += mul(get(gain, g, x), force)
+        return state
+
+    def parcel(g, target):
+        return pltpu.make_async_remote_copy(
+            src_ref=given.at[g, target],
+            dst_ref=taken.at[g, gx],
+            send_sem=vec_send.at[g, target],
+            recv_sem=vec_recv.at[g, gx],
+            device_id=(target, yz),
+            device_id_type=MESH,
+        )
+
+    def receive(g, source):
+        pltpu.make_async_remote_copy(
+            src_ref=given.at[g, source],
+            dst_ref=taken.at[g, source],
+            send_sem=vec_send.at[g, source],
+            recv_sem=vec_recv.at[g, source],
+            device_id=(source, yz),
+            device_id_type=MESH,
+        ).wait_recv()
+
+    def dispatch(g):
+        ah, al = split(acc[g])
+        for t in range(n_gx // 4):
+            zh = send_map[g, 0, 4 * t : 4 * t + 4].reshape(4 * nv, 2 * nv)
+            zl = send_map[g, 1, 4 * t : 4 * t + 4].reshape(4 * nv, 2 * nv)
+            given[g, 4 * t : 4 * t + 4] = mul((zh, zl), (ah, al)).reshape(4, nv, nz)
+        for k in range(1, n_gx):
+            parcel(g, lax.rem(gx + k, n_gx)).start()
+
+    def local_backward(g):
+        into_state[g] = cs[g, cells - 1]
 
         def backward(i, carry):
             x = cells - 2 - i
-            for g in range(groups):
-                state = cs[g, x] + mul(get(bt, g, x), split(into_state[g]))
-                into_state[g] = state
-                cs[g, x] = state
+            state = cs[g, x] + mul(get(bt, g, x), split(into_state[g]))
+            into_state[g] = state
+            cs[g, x] = state
             return carry
 
         lax.fori_loop(0, cells - 1, backward, 0)
 
     def finish(g):
-        total = jnp.zeros((2 * nv, nz), F32)
-        tail = jnp.zeros((nv, nz), F32)
-        for j in range(n_gx):
-            total = total + mul(get(wc, g, j), split(gvec[g, j, :nv]))
-            tail = tail + mul(get(wl, g, j), split(gvec[g, j, nv:]))
-        into[g, 0, :nv], into[g, 1, :nv] = split(total[:nv])
-        into[g, 0, nv:], into[g, 1, nv:] = split(total[nv:] + tail)
-
-        def fix(x, carry):
-            value = cs[g, x] + mul(get(resp, g, x), (into[g, 0], into[g, 1]))
-            out[x, g] = jnp.where(cat[x][g : g + 1] != 1, value, 0.0)
-            return carry
-
-        loop(cells, fix, 0, 4)
-
-    local_forward(0)
-    offer(*vecs[0])
+        head = jnp.zeros((nv, nz), F32)
+        tail = given[g, gx]
+        for k in range(1, n_gx):
+            j = lax.rem(gx + k, n_gx)
+            receive(g, j)
+            value = taken[g, j]
+            head = head + jnp.where(j < gx, value, 0.0)
+            tail = tail + jnp.where(j < gx, 0.0, value)
+        both = split(jnp.concatenate([head, tail], axis=0))
+        block = next(c for c in (4, 3, 2, 1) if cells % c == 0)
+        for x in range(0, cells, block):
+            maps_here = tuple(
+                resp[g, n, x : x + block].reshape(block * nv, 2 * nv) for n in range(2)
+            )
+            fix = mul(maps_here, both).reshape(block, nv, nz)
+            for k in range(block):
+                value = cs[g, x + k] + fix[k]
+                out[x + k, g] = jnp.where(cat[x + k][g : g + 1] != 1, value, 0.0)
+
+    for g in range(groups):
+        acc[g] = jnp.zeros((2 * nv, nz), F32)
+
+    state = jnp.zeros((nv, nz), F32)
+    for c in range(pieces):
+        arrive(0, c)
+        state = local_forward(0, c, state, True)
+
     relay(*maps)
     collect(*maps)
 
     for g in range(groups):
-        side[g] = jnp.zeros((nv, nv), F32)
-        tall[g] = jnp.zeros((2 * nv, nv), F32)
-
-    def suffix(j, carry):
-        here = jnp.where(gx == j, 1.0, 0.0)
+        mirror[g] = jnp.zeros((nv, nv), F32)
+        ahead[g, 0] = unit
+        behind[g, n_gx] = unit
+
+    def chains(t, carry):
+        i = n_gx - 1 - t
+        p_up = gmap[t, groups * nv :]
+        p_down = gmap[i, groups * nv :]
+        grow = t > gx
+        shrink = i < gx
+        here = i == gx
         for g in range(groups):
-            e = split(side[g])
-            put(wl, g, j, e)
-            both = mul(e, split(gmap[j, g * nv : (g + 1) * nv]))
-            side[g] = both[:, nv:] + here * unit
-            hom[g, j] = both
+            cols = slice(g * nv, (g + 1) * nv)
+            step = mul(split(p_up[:, cols]), split(ahead[g, t]))
+            ahead[g, t + 1] = jnp.where(grow, step, unit)
+            rq = gmap[i, g * nv : (g + 1) * nv]
+            q = split(rq[:, nv:])
+            step = mul(q, split(behind[g, i + 1]))
+            behind[g, i] = jnp.where(shrink, step, unit)
+            s_now = mirror[g]
+            qs = mul(q, split(s_now))
+            hom[g, i] = jnp.concatenate([qs, s_now], axis=1)
+            mirror[g] = rq[:, :nv] + mul(split(qs), split(p_down[:, cols]))
         return carry
 
-    loop(n_gx, suffix, 0)
-
-    def prefix(i, carry):
-        j = n_gx - 1 - i
-        here = jnp.where(gx == j, 1.0, 0.0)
-        maps_here = gmap[j, groups * nv :]
-        for g in range(groups):
-            xs = split(tall[g])
-            put(wc, g, j, xs)
-            nxt = mul(xs, split(maps_here[:, g * nv : (g + 1) * nv]))
-            tall[g, :nv] = nxt[:nv] + here * unit
-            tall[g, nv:] = nxt[nv:] + hom[g, j][:, :nv]
-        return carry
-
-    loop(n_gx, prefix, 0)
-
-    relay(*vecs[0])
-    for g in range(1, groups):
-        local_forward(g)
-        offer(*vecs[g])
-    local_backward()
-    for g in range(1, groups):
-        relay(*vecs[g])
-    for g in range(groups):
-        collect(*vecs[g])
+    loop(n_gx, chains, 0)
+
+    for g in range(groups):
+        pair = hom[g, gx]
+        qs = pair[:, :nv]
+        s_now = pair[:, nv:]
+        zero = jnp.zeros((nv, nv), F32)
+        p_here = gmap[gx, groups * nv :][:, g * nv : (g + 1) * nv]
+        sp = mul(split(s_now), split(p_here))
+        left = jnp.concatenate([qs, unit], axis=1)
+        for i in range(n_gx):
+            m = mul(split(behind[g, i + 1]), split(left))
+            m = jnp.where(i < gx, m, jnp.concatenate([ahead[g, i], zero], axis=1))
+            m = jnp.where(gx == i, jnp.concatenate([s_now, zero], axis=1), m)
+            send_map[g, 0, i], send_map[g, 1, i] = split(m)
+        turn = split(
+            jnp.concatenate(
+                [first_unit, jnp.concatenate([sp, unit], axis=1)], axis=0
+            )
+        )
+        block = next(c for c in (4, 3, 2, 1) if cells % c == 0)
+        for x in range(0, cells, block):
+            maps_here = tuple(
+                resp[g, n, x : x + block].reshape(block * nv, 2 * nv) for n in range(2)
+            )
+            fixed = split(mul(maps_here, turn))
+            for n in range(2):
+                resp[g, n, x : x + block] = fixed[n].reshape(block, nv, 2 * nv)
+
+    dispatch(0)
+    local_backward(0)
+
+    last = groups - 1
+    for n in range(chunk):
+        x = edge + n
+        fast[n, 0], fast[n, 1] = split(mul(get(gain, last, x), held(last, 0)))
+        acc[last] += mul(get(gain, last, x), split(weight(last, x) * res[x, last]))
+
+    state = jnp.zeros((nv, nz), F32)
+    for c in range(pieces - 1):
+        arrive(last, c)
+        state = local_forward(last, c, state, True)
+    arrive(last, pieces - 1)
+    for n in range(chunk):
+        x = edge + n
+        acc[last] += mul((fast[n, 0], fast[n, 1]), split(weight(last, x) * slope(last, x)))
+    dispatch(last)
+    local_forward(last, pieces - 1, state, False)
+    local_backward(last)
+    for g in range(groups):
         finish(g)
 
     @pl.when(has_high)
@@ -357,7 +434,8 @@
 
     release(*maps)
     for g in range(groups):
-        release(*vecs[g])
+        for k in range(1, n_gx):
+            parcel(g, lax.rem(gx + k, n_gx)).wait_send()
 
 
 def per_device(n_gx, n_yz, residual, inverses, upwind, downwind, flux_y, kinds, volume_category):
@@ -385,14 +463,17 @@
             square,
             pltpu.VMEM((groups, max(cells, n_gx) + 1, nv, 2 * nv), F32),
             pltpu.VMEM((groups, cells + 1, nv, nv), F32),
-            square,
-            pltpu.VMEM((groups, cells, 2, nv, 2 * nv), BF16),
+            pltpu.VMEM((groups, cells, 2, 2 * nv, nv), BF16),
+            pltpu.VMEM((chunk, 2, 2 * nv, nv), BF16),
+            pltpu.VMEM((groups, 2, cells, nv, 2 * nv), BF16),
             wide,
+            pltpu.VMEM((groups, 2 * nv, nz), F32),
             pltpu.VMEM((n_gx, (groups + 1) * nv, 2 * nv), F32),
-            pltpu.VMEM((groups, n_gx, 2 * nv, nz), F32),
-            pltpu.VMEM((groups, n_gx, 2, 2 * nv, nv), BF16),
-            pltpu.VMEM((groups, n_gx, 2, nv, nv), BF16),
-            pltpu.VMEM((groups, 2, 2 * nv, nz), BF16),
+            pltpu.VMEM((groups, n_gx, nv, nz), F32),
+            pltpu.VMEM((groups, n_gx, nv, nz), F32),
+            pltpu.VMEM((groups, 2, n_gx, nv, 2 * nv), BF16),
+            pltpu.VMEM((groups, n_gx + 1, nv, nv), F32),
+            pltpu.VMEM((groups, n_gx + 1, nv, nv), F32),
             pltpu.VMEM((groups, nv, nv), F32),
             pltpu.VMEM((groups, nv, 2 * nv), F32),
             pltpu.VMEM((groups, 2 * nv, nv), F32),

time: 32.7 us -> 34.2 us (1.046)
  Pallas kernels: 31.7 us -> 33.2 us
    pallas_call x1, Pallas kernels: 31.7 us -> 33.2 us  [per_device(): pl.pallas_call(functools.partial(kernel, n_gx, n_yz, chunk), out_shape=ja...]
where the time goes in v1:
time: 34.2 us; the launch traced here: 34.1 us
  Pallas kernels  33.2 us (97%)
  local copies, waits for them, and re-layouts  0.88 us (3%)
    pallas_call x1, Pallas kernels, per_device(): pl.pallas_call(functools.partial(kernel, n_gx, n_yz, chunk), out_shape=ja...  33.2 us
    unnamed x1, local copies, waits for them, and re-layouts  0.88 us

profile of v1, /device:TPU:0, one launch (start us, length us, event | category | flops | bytes accessed | tf_op | source)
XLA Modules:
  0.0 34.1 jit_solution(7612577967071029768)
XLA Ops:
  0.0 33.2 %shard_map.73 = f32[12,2,64,128]{3,2,1,0:T(8,128)S(1)} custom-call(f32[12,2,64,128]{3,2,1,0:T(8,128)} %res_hbm.1, f32[12,2,64,64]{3,2,1,0:T(8,128)} %inv_hbm.1, f32[8,64,64]{2,1,0:T(8,128)} %up_hbm.1, f32[8,64,64]{2,1,0:T(8,128)} %down_hbm.1, f32[8,64,64]{2,1,0:T(8,128)} %flux_hbm.1, s32[12,2,128]{2,1,0:T(2,128)} %cat_hbm.1, s32[2]{0:T(128)} %kinds_hbm.1), custom_call_target="tpu_custom_call" | custom-call | tf_op jit(solution)/shard_map/pallas_call | solution.py:449
  33.2 0.9 %copy.9 = f32[12,2,64,128]{3,2,1,0:T(8,128)} copy(f32[12,2,64,128]{3,2,1,0:T(8,128)S(1)} %shard_map.73) | data formatting | bytes 1572864

commit v2 on v1

--- a/solution.py
+++ b/solution.py
@@ -38,7 +38,7 @@
 def kernel(
     n_gx, n_yz, chunk, res_hbm, inv_hbm, up_hbm, down_hbm, flux_hbm, cat_hbm, kinds_hbm, out,
     res, inv, up, down, flux, cat, kinds,
-    snd, low, high, table, vt, ft, bt, hom, omega, gain, fast, resp, cs, acc, gmap, given, taken,
+    snd, low, high, table, vt, ft, bt, hom, omega, path, echo, gain, fast, resp, cs, acc, gmap, given, taken,
     send_map, ahead, behind, mirror, wide_state, tall, into_state,
     load_sem, halo_send, halo_recv, map_send, map_recv, vec_send, vec_recv,
 ):
@@ -172,14 +172,65 @@
     for g in range(groups):
         hom[g, 0] = first_unit
         omega[g, 0] = unit
+        path[g] = jnp.zeros((2, nv, nv), BF16)
+        echo[g] = jnp.zeros((nv, 2 * nv), F32)
 
     def hom_forward(x, carry):
         for g in range(groups):
-            hom[g, x + 1] = mul(get(ft, g, x), split(hom[g, x]))
-            omega[g, x + 1] = mul(split(omega[g, x]), get(bt, g, x))
+            onward = split(omega[g, x])
+            ahead_of = tuple(
+                jnp.concatenate([ft[g, x, n], path[g, n]], axis=0) for n in range(2)
+            )
+            both = mul(ahead_of, split(hom[g, x]))
+            hom[g, x + 1] = both[:nv]
+            echo[g] += both[nv:]
+            omega[g, x + 1] = mul(onward, get(bt, g, x))
+            path[g, 0], path[g, 1] = onward
         return carry
 
     loop(cells, hom_forward, 0)
+    for g in range(groups):
+        total = echo[g] + mul((path[g, 0], path[g, 1]), split(hom[g, cells]))
+        gmap[gx, g * nv : (g + 1) * nv] = jnp.concatenate(
+            [total[:, :nv], omega[g, cells]], axis=1
+        )
+    gmap[gx, groups * nv :] = jnp.concatenate(
+        [hom[g, cells][:, :nv] for g in range(groups)], axis=1
+    )
+
+    def share(buffer, send, recv, slot, target, k):
+        return pltpu.make_async_remote_copy(
+            src_ref=buffer.at[slot],
+            dst_ref=buffer.at[slot],
+            send_sem=send.at[k],
+            recv_sem=recv.at[slot],
+            device_id=(target, yz),
+            device_id_type=MESH,
+        )
+
+    def offer(*where):
+        for k in range(1, half):
+            share(*where, gx, peer(k), k).start()
+        share(*where, gx, partner, 0).start()
+
+    def relay(*where):
+        for k in range(1, half):
+            share(*where, peer(k), peer(k), k).wait_recv()
+            share(*where, peer(k), partner, half + k).start()
+
+    def collect(*where):
+        share(*where, partner, partner, 0).wait_recv()
+        for k in range(1, half):
+            share(*where, lax.rem(partner + 2 * k, n_gx), partner, half + k).wait_recv()
+
+    def release(*where):
+        share(*where, gx, partner, 0).wait_send()
+        for k in range(1, half):
+            share(*where, gx, peer(k), k).wait_send()
+            share(*where, peer(k), partner, half + k).wait_send()
+
+    maps = (gmap, map_send, map_recv)
+    offer(*maps)
 
     for g in range(groups):
         tall[g, :nv] = unit
@@ -200,45 +251,6 @@
         return carry
 
     loop(cells, hom_backward, 0)
-    for g in range(groups):
-        gmap[gx, g * nv : (g + 1) * nv] = wide_state[g]
-    gmap[gx, groups * nv :] = jnp.concatenate(
-        [hom[g, cells][:, :nv] for g in range(groups)], axis=1
-    )
-
-    def share(buffer, send, recv, slot, target, k):
-        return pltpu.make_async_remote_copy(
-            src_ref=buffer.at[slot],
-            dst_ref=buffer.at[slot],
-            send_sem=send.at[k],
-            recv_sem=recv.at[slot],
-            device_id=(target, yz),
-            device_id_type=MESH,
-        )
-
-    def offer(*where):
-        for k in range(1, half):
-            share(*where, gx, peer(k), k).start()
-        share(*where, gx, partner, 0).start()
-
-    def relay(*where):
-        for k in range(1, half):
-            share(*where, peer(k), peer(k), k).wait_recv()
-            share(*where, peer(k), partner, half + k).start()
-
-    def collect(*where):
-        share(*where, partner, partner, 0).wait_recv()
-        for k in range(1, half):
-            share(*where, lax.rem(partner + 2 * k, n_gx), partner, half + k).wait_recv()
-
-    def release(*where):
-        share(*where, gx, partner, 0).wait_send()
-        for k in range(1, half):
-            share(*where, gx, peer(k), k).wait_send()
-            share(*where, peer(k), partner, half + k).wait_send()
-
-    maps = (gmap, map_send, map_recv)
-    offer(*maps)
 
     edge = cells - chunk
 
@@ -260,15 +272,12 @@
         def _():
             halo(1, g, c).wait_recv()
 
-    def local_forward(g, c, state, gather):
+    def local_forward(g, c, gather):
         for x in range(c * chunk, (c + 1) * chunk):
             force = split(weight(g, x) * (res[x, g] + mul(held(g, 0), split(slope(g, x)))))
-            driven = mul(get(vt, g, x), force)
-            state = driven + mul(get(ft, g, x), split(state))
-            cs[g, x] = state
+            cs[g, x] = mul(get(vt, g, x), force)
             if gather:
                 acc[g] += mul(get(gain, g, x), force)
-        return state
 
     def parcel(g, target):
         return pltpu.make_async_remote_copy(
@@ -299,14 +308,25 @@
         for k in range(1, n_gx):
             parcel(g, lax.rem(gx + k, n_gx)).start()
 
-    def local_backward(g):
-        into_state[g] = cs[g, cells - 1]
+    def sweep():
+        for g in range(groups):
+            into_state[g] = cs[g, 0]
+
+        def forward(i, carry):
+            for g in range(groups):
+                state = cs[g, i + 1] + mul(get(ft, g, i + 1), split(into_state[g]))
+                into_state[g] = state
+                cs[g, i + 1] = state
+            return carry
+
+        lax.fori_loop(0, cells - 1, forward, 0)
 
         def backward(i, carry):
             x = cells - 2 - i
-            state = cs[g, x] + mul(get(bt, g, x), split(into_state[g]))
-            into_state[g] = state
-            cs[g, x] = state
+            for g in range(groups):
+                state = cs[g, x] + mul(get(bt, g, x), split(into_state[g]))
+                into_state[g] = state
+                cs[g, x] = state
             return carry
 
         lax.fori_loop(0, cells - 1, backward, 0)
@@ -334,10 +354,9 @@
     for g in range(groups):
         acc[g] = jnp.zeros((2 * nv, nz), F32)
 
-    state = jnp.zeros((nv, nz), F32)
     for c in range(pieces):
         arrive(0, c)
-        state = local_forward(0, c, state, True)
+        local_forward(0, c, True)
 
     relay(*maps)
     collect(*maps)
@@ -398,7 +417,6 @@
                 resp[g, n, x : x + block] = fixed[n].reshape(block, nv, 2 * nv)
 
     dispatch(0)
-    local_backward(0)
 
     last = groups - 1
     for n in range(chunk):
@@ -406,17 +424,16 @@
         fast[n, 0], fast[n, 1] = split(mul(get(gain, last, x), held(last, 0)))
         acc[last] += mul(get(gain, last, x), split(weight(last, x) * res[x, last]))
 
-    state = jnp.zeros((nv, nz), F32)
     for c in range(pieces - 1):
         arrive(last, c)
-        state = local_forward(last, c, state, True)
+        local_forward(last, c, True)
     arrive(last, pieces - 1)
     for n in range(chunk):
         x = edge + n
         acc[last] += mul((fast[n, 0], fast[n, 1]), split(weight(last, x) * slope(last, x)))
     dispatch(last)
-    local_forward(last, pieces - 1, state, False)
-    local_backward(last)
+    local_forward(last, pieces - 1, False)
+    sweep()
     for g in range(groups):
         finish(g)
 
@@ -463,6 +480,8 @@
             square,
             pltpu.VMEM((groups, max(cells, n_gx) + 1, nv, 2 * nv), F32),
             pltpu.VMEM((groups, cells + 1, nv, nv), F32),
+            pltpu.VMEM((groups, 2, nv, nv), BF16),
+            pltpu.VMEM((groups, nv, 2 * nv), F32),
             pltpu.VMEM((groups, cells, 2, 2 * nv, nv), BF16),
             pltpu.VMEM((chunk, 2, 2 * nv, nv), BF16),
             pltpu.VMEM((groups, 2, cells, nv, 2 * nv), BF16),

time: 34.2 us -> 31.3 us (0.915); the launches traced: 34.1 us -> 30.8 us
  Pallas kernels: 33.2 us -> 29.9 us
    pallas_call x1, Pallas kernels: 33.2 us -> 29.9 us  [per_device(): pl.pallas_call(functools.partial(kernel, n_gx, n_yz, chunk), out_shape=ja...]
where the time goes in v2:
time: 31.3 us; the launch traced here: 30.8 us
  Pallas kernels  29.9 us (96%)
  local copies, waits for them, and re-layouts  0.88 us (3%)
    pallas_call x1, Pallas kernels, per_device(): pl.pallas_call(functools.partial(kernel, n_gx, n_yz, chunk), out_shape=ja...  29.9 us
    unnamed x1, local copies, waits for them, and re-layouts  0.88 us

profile of v2, /device:TPU:0, one launch (start us, length us, event | category | flops | bytes accessed | tf_op | source)
XLA Modules:
  0.0 30.8 jit_solution(6369914762366949419)
XLA Ops:
  0.0 29.9 %shard_map.73 = f32[12,2,64,128]{3,2,1,0:T(8,128)S(1)} custom-call(f32[12,2,64,128]{3,2,1,0:T(8,128)} %res_hbm.1, f32[12,2,64,64]{3,2,1,0:T(8,128)} %inv_hbm.1, f32[8,64,64]{2,1,0:T(8,128)} %up_hbm.1, f32[8,64,64]{2,1,0:T(8,128)} %down_hbm.1, f32[8,64,64]{2,1,0:T(8,128)} %flux_hbm.1, s32[12,2,128]{2,1,0:T(2,128)} %cat_hbm.1, s32[2]{0:T(128)} %kinds_hbm.1), custom_call_target="tpu_custom_call" | custom-call | tf_op jit(solution)/shard_map/pallas_call | solution.py:466
  29.9 0.9 %copy.9 = f32[12,2,64,128]{3,2,1,0:T(8,128)} copy(f32[12,2,64,128]{3,2,1,0:T(8,128)S(1)} %shard_map.73) | data formatting | bytes 1572864

commit v3 on v2

--- a/solution.py
+++ b/solution.py
@@ -253,6 +253,7 @@
     loop(cells, hom_backward, 0)
 
     edge = cells - chunk
+    block = next(c for c in (12, 6, 4, 3, 2, 1) if cells % c == 0)
 
     def weight(g, x):
         kind = cat[x][g : g + 1]
@@ -272,12 +273,17 @@
         def _():
             halo(1, g, c).wait_recv()
 
-    def local_forward(g, c, gather):
-        for x in range(c * chunk, (c + 1) * chunk):
-            force = split(weight(g, x) * (res[x, g] + mul(held(g, 0), split(slope(g, x)))))
+    def local_forward(g, first, count, gather):
+        xs = range(first, first + count)
+        flux_in = [mul(held(g, 0), split(slope(g, x))) for x in xs]
+        forces = [split(weight(g, x) * (res[x, g] + f)) for x, f in zip(xs, flux_in)]
+        if gather:
+            total = acc[g]
+            for x, force in zip(xs, forces):
+                total = total + mul(get(gain, g, x), force)
+            acc[g] = total
+        for x, force in zip(xs, forces):
             cs[g, x] = mul(get(vt, g, x), force)
-            if gather:
-                acc[g] += mul(get(gain, g, x), force)
 
     def parcel(g, target):
         return pltpu.make_async_remote_copy(
@@ -341,13 +347,13 @@
             head = head + jnp.where(j < gx, value, 0.0)
             tail = tail + jnp.where(j < gx, 0.0, value)
         both = split(jnp.concatenate([head, tail], axis=0))
-        block = next(c for c in (4, 3, 2, 1) if cells % c == 0)
-        for x in range(0, cells, block):
+        high_block = next(c for c in (4, 3, 2, 1) if cells % c == 0)
+        for x in range(0, cells, high_block):
             maps_here = tuple(
-                resp[g, n, x : x + block].reshape(block * nv, 2 * nv) for n in range(2)
+                resp[g, n, x : x + high_block].reshape(high_block * nv, 2 * nv) for n in range(2)
             )
-            fix = mul(maps_here, both).reshape(block, nv, nz)
-            for k in range(block):
+            fix = mul(maps_here, both).reshape(high_block, nv, nz)
+            for k in range(high_block):
                 value = cs[g, x + k] + fix[k]
                 out[x + k, g] = jnp.where(cat[x + k][g : g + 1] != 1, value, 0.0)
 
@@ -356,45 +362,43 @@
 
     for c in range(pieces):
         arrive(0, c)
-        local_forward(0, c, True)
+    for x in range(0, cells, block):
+        local_forward(0, x, block, True)
 
     relay(*maps)
     collect(*maps)
 
     for g in range(groups):
-        mirror[g] = jnp.zeros((nv, nv), F32)
         ahead[g, 0] = unit
         behind[g, n_gx] = unit
+        mirror[g, 0] = unit
 
     def chains(t, carry):
         i = n_gx - 1 - t
         p_up = gmap[t, groups * nv :]
-        p_down = gmap[i, groups * nv :]
         grow = t > gx
         shrink = i < gx
-        here = i == gx
-        for g in range(groups):
-            cols = slice(g * nv, (g + 1) * nv)
-            step = mul(split(p_up[:, cols]), split(ahead[g, t]))
+        for g in range(groups):
+            rows = slice(g * nv, (g + 1) * nv)
+            step = mul(split(p_up[:, rows]), split(ahead[g, t]))
             ahead[g, t + 1] = jnp.where(grow, step, unit)
-            rq = gmap[i, g * nv : (g + 1) * nv]
-            q = split(rq[:, nv:])
-            step = mul(q, split(behind[g, i + 1]))
+            step = mul(split(gmap[i, rows][:, nv:]), split(behind[g, i + 1]))
             behind[g, i] = jnp.where(shrink, step, unit)
-            s_now = mirror[g]
-            qs = mul(q, split(s_now))
-            hom[g, i] = jnp.concatenate([qs, s_now], axis=1)
-            mirror[g] = rq[:, :nv] + mul(split(qs), split(p_down[:, cols]))
+            step = mul(split(mirror[g, t]), split(gmap[t, rows][:, nv:]))
+            mirror[g, t + 1] = jnp.where(grow, step, unit)
         return carry
 
     loop(n_gx, chains, 0)
 
     for g in range(groups):
-        pair = hom[g, gx]
-        qs = pair[:, :nv]
-        s_now = pair[:, nv:]
+        rows = slice(g * nv, (g + 1) * nv)
+        s_now = jnp.zeros((nv, nv), F32)
+        inner = [mul(split(gmap[j, rows][:, :nv]), split(ahead[g, j])) for j in range(1, n_gx)]
+        for j in range(1, n_gx):
+            s_now = s_now + jnp.where(j > gx, mul(split(mirror[g, j]), split(inner[j - 1])), 0.0)
         zero = jnp.zeros((nv, nv), F32)
-        p_here = gmap[gx, groups * nv :][:, g * nv : (g + 1) * nv]
+        qs = mul(split(gmap[gx, rows][:, nv:]), split(s_now))
+        p_here = gmap[gx, groups * nv :][:, rows]
         sp = mul(split(s_now), split(p_here))
         left = jnp.concatenate([qs, unit], axis=1)
         for i in range(n_gx):
@@ -407,14 +411,14 @@
                 [first_unit, jnp.concatenate([sp, unit], axis=1)], axis=0
             )
         )
-        block = next(c for c in (4, 3, 2, 1) if cells % c == 0)
-        for x in range(0, cells, block):
+        high_block = next(c for c in (4, 3, 2, 1) if cells % c == 0)
+        for x in range(0, cells, high_block):
             maps_here = tuple(
-                resp[g, n, x : x + block].reshape(block * nv, 2 * nv) for n in range(2)
+                resp[g, n, x : x + high_block].reshape(high_block * nv, 2 * nv) for n in range(2)
             )
             fixed = split(mul(maps_here, turn))
             for n in range(2):
-                resp[g, n, x : x + block] = fixed[n].reshape(block, nv, 2 * nv)
+                resp[g, n, x : x + high_block] = fixed[n].reshape(high_block, nv, 2 * nv)
 
     dispatch(0)
 
@@ -426,13 +430,14 @@
 
     for c in range(pieces - 1):
         arrive(last, c)
-        local_forward(last, c, True)
+    for x in range(0, edge, min(edge, 9)):
+        local_forward(last, x, min(9, edge - x), True)
     arrive(last, pieces - 1)
     for n in range(chunk):
         x = edge + n
         acc[last] += mul((fast[n, 0], fast[n, 1]), split(weight(last, x) * slope(last, x)))
     dispatch(last)
-    local_forward(last, pieces - 1, False)
+    local_forward(last, edge, chunk, False)
     sweep()
     for g in range(groups):
         finish(g)
@@ -493,7 +498,7 @@
             pltpu.VMEM((groups, 2, n_gx, nv, 2 * nv), BF16),
             pltpu.VMEM((groups, n_gx + 1, nv, nv), F32),
             pltpu.VMEM((groups, n_gx + 1, nv, nv), F32),
-            pltpu.VMEM((groups, nv, nv), F32),
+            pltpu.VMEM((groups, n_gx + 1, nv, nv), F32),
             pltpu.VMEM((groups, nv, 2 * nv), F32),
             pltpu.VMEM((groups, 2 * nv, nv), F32),
             pltpu.VMEM((groups, nv, nz), F32),

time: 31.3 us -> 31.1 us (level); the launches traced: 30.8 us -> 30.9 us
  no operation moved by 1% of the time
where the time goes in v3:
time: 31.1 us; the launch traced here: 30.9 us
  Pallas kernels  30 us (96%)
  local copies, waits for them, and re-layouts  0.88 us (3%)
    pallas_call x1, Pallas kernels, per_device(): pl.pallas_call(functools.partial(kernel, n_gx, n_yz, chunk), out_shape=ja...  30 us
    unnamed x1, local copies, waits for them, and re-layouts  0.88 us

profile of v3, /device:TPU:0, one launch (start us, length us, event | category | flops | bytes accessed | tf_op | source)
XLA Modules:
  0.0 30.9 jit_solution(610517449443895572)
XLA Ops:
  0.0 30.0 %shard_map.73 = f32[12,2,64,128]{3,2,1,0:T(8,128)S(1)} custom-call(f32[12,2,64,128]{3,2,1,0:T(8,128)} %res_hbm.1, f32[12,2,64,64]{3,2,1,0:T(8,128)} %inv_hbm.1, f32[8,64,64]{2,1,0:T(8,128)} %up_hbm.1, f32[8,64,64]{2,1,0:T(8,128)} %down_hbm.1, f32[8,64,64]{2,1,0:T(8,128)} %flux_hbm.1, s32[12,2,128]{2,1,0:T(2,128)} %cat_hbm.1, s32[2]{0:T(128)} %kinds_hbm.1), custom_call_target="tpu_custom_call" | custom-call | tf_op jit(solution)/shard_map/pallas_call | solution.py:471
  30.1 0.9 %copy.9 = f32[12,2,64,128]{3,2,1,0:T(8,128)} copy(f32[12,2,64,128]{3,2,1,0:T(8,128)S(1)} %shard_map.73) | data formatting | bytes 1572864

commit v4 on v3

--- a/solution.py
+++ b/solution.py
@@ -39,7 +39,7 @@
     n_gx, n_yz, chunk, res_hbm, inv_hbm, up_hbm, down_hbm, flux_hbm, cat_hbm, kinds_hbm, out,
     res, inv, up, down, flux, cat, kinds,
     snd, low, high, table, vt, ft, bt, hom, omega, path, echo, gain, fast, resp, cs, acc, gmap, given, taken,
-    send_map, ahead, behind, mirror, wide_state, tall, into_state,
+    send_map, ahead, behind, mirror, side, wide_state, tall, into_state,
     load_sem, halo_send, halo_recv, map_send, map_recv, vec_send, vec_recv,
 ):
     cells, groups, nv, nz = res.shape
@@ -314,28 +314,28 @@
         for k in range(1, n_gx):
             parcel(g, lax.rem(gx + k, n_gx)).start()
 
-    def sweep():
-        for g in range(groups):
-            into_state[g] = cs[g, 0]
-
+    def sweep_forward(g, first, count):
         def forward(i, carry):
-            for g in range(groups):
-                state = cs[g, i + 1] + mul(get(ft, g, i + 1), split(into_state[g]))
-                into_state[g] = state
-                cs[g, i + 1] = state
+            state = cs[g, i] + mul(get(ft, g, i), split(into_state[g]))
+            into_state[g] = state
+            cs[g, i] = state
             return carry
 
-        lax.fori_loop(0, cells - 1, forward, 0)
+        lax.fori_loop(first, first + count, forward, 0)
+
+    def sweep_backward():
+        for g in range(groups):
+            into_state[g] = jnp.zeros((nv, nz), F32)
 
         def backward(i, carry):
-            x = cells - 2 - i
+            x = cells - 1 - i
             for g in range(groups):
                 state = cs[g, x] + mul(get(bt, g, x), split(into_state[g]))
                 into_state[g] = state
                 cs[g, x] = state
             return carry
 
-        lax.fori_loop(0, cells - 1, backward, 0)
+        lax.fori_loop(0, cells, backward, 0)
 
     def finish(g):
         head = jnp.zeros((nv, nz), F32)
@@ -357,6 +357,22 @@
                 value = cs[g, x + k] + fix[k]
                 out[x + k, g] = jnp.where(cat[x + k][g : g + 1] != 1, value, 0.0)
 
+    def turned(g):
+        sp = side[g]
+        turn = split(
+            jnp.concatenate(
+                [first_unit, jnp.concatenate([sp, unit], axis=1)], axis=0
+            )
+        )
+        high_block = next(c for c in (4, 3, 2, 1) if cells % c == 0)
+        for x in range(0, cells, high_block):
+            maps_here = tuple(
+                resp[g, n, x : x + high_block].reshape(high_block * nv, 2 * nv) for n in range(2)
+            )
+            fixed = split(mul(maps_here, turn))
+            for n in range(2):
+                resp[g, n, x : x + high_block] = fixed[n].reshape(high_block, nv, 2 * nv)
+
     for g in range(groups):
         acc[g] = jnp.zeros((2 * nv, nz), F32)
 
@@ -365,15 +381,30 @@
     for x in range(0, cells, block):
         local_forward(0, x, block, True)
 
+    last = groups - 1
+    for n in range(chunk):
+        x = edge + n
+        fast[n, 0], fast[n, 1] = split(mul(get(gain, last, x), held(last, 0)))
+        acc[last] += mul(get(gain, last, x), split(weight(last, x) * res[x, last]))
+    for g in range(groups):
+        into_state[g] = jnp.zeros((nv, nz), F32)
+    sweep_forward(0, 0, cells)
+
     relay(*maps)
+    first_wave = chunk if pieces > 1 else 0
+    if first_wave:
+        arrive(last, 0)
+        local_forward(last, 0, chunk, True)
     collect(*maps)
 
     for g in range(groups):
-        ahead[g, 0] = unit
-        behind[g, n_gx] = unit
-        mirror[g, 0] = unit
-
-    def chains(t, carry):
+        for t in range(2):
+            ahead[g, t] = unit
+            behind[g, n_gx - t] = unit
+            mirror[g, t] = unit
+
+    def chains(n, carry):
+        t = n + 1
         i = n_gx - 1 - t
         p_up = gmap[t, groups * nv :]
         grow = t > gx
@@ -388,7 +419,7 @@
             mirror[g, t + 1] = jnp.where(grow, step, unit)
         return carry
 
-    loop(n_gx, chains, 0)
+    loop(n_gx - 2, chains, 0)
 
     for g in range(groups):
         rows = slice(g * nv, (g + 1) * nv)
@@ -406,39 +437,25 @@
             m = jnp.where(i < gx, m, jnp.concatenate([ahead[g, i], zero], axis=1))
             m = jnp.where(gx == i, jnp.concatenate([s_now, zero], axis=1), m)
             send_map[g, 0, i], send_map[g, 1, i] = split(m)
-        turn = split(
-            jnp.concatenate(
-                [first_unit, jnp.concatenate([sp, unit], axis=1)], axis=0
-            )
-        )
-        high_block = next(c for c in (4, 3, 2, 1) if cells % c == 0)
-        for x in range(0, cells, high_block):
-            maps_here = tuple(
-                resp[g, n, x : x + high_block].reshape(high_block * nv, 2 * nv) for n in range(2)
-            )
-            fixed = split(mul(maps_here, turn))
-            for n in range(2):
-                resp[g, n, x : x + high_block] = fixed[n].reshape(high_block, nv, 2 * nv)
+        side[g] = sp
 
     dispatch(0)
 
-    last = groups - 1
-    for n in range(chunk):
-        x = edge + n
-        fast[n, 0], fast[n, 1] = split(mul(get(gain, last, x), held(last, 0)))
-        acc[last] += mul(get(gain, last, x), split(weight(last, x) * res[x, last]))
-
-    for c in range(pieces - 1):
+    for c in range(1, pieces - 1):
         arrive(last, c)
-    for x in range(0, edge, min(edge, 9)):
-        local_forward(last, x, min(9, edge - x), True)
+    for x in range(first_wave, edge, 6):
+        local_forward(last, x, min(6, edge - x), True)
     arrive(last, pieces - 1)
     for n in range(chunk):
         x = edge + n
         acc[last] += mul((fast[n, 0], fast[n, 1]), split(weight(last, x) * slope(last, x)))
     dispatch(last)
     local_forward(last, edge, chunk, False)
-    sweep()
+    for g in range(1, groups):
+        sweep_forward(g, 0, cells)
+    sweep_backward()
+    for g in range(groups):
+        turned(g)
     for g in range(groups):
         finish(g)
 
@@ -499,6 +516,7 @@
             pltpu.VMEM((groups, n_gx + 1, nv, nv), F32),
             pltpu.VMEM((groups, n_gx + 1, nv, nv), F32),
             pltpu.VMEM((groups, n_gx + 1, nv, nv), F32),
+            pltpu.VMEM((groups, nv, nv), F32),
             pltpu.VMEM((groups, nv, 2 * nv), F32),
             pltpu.VMEM((groups, 2 * nv, nv), F32),
             pltpu.VMEM((groups, nv, nz), F32),

time: 31.1 us -> 32.4 us (1.042)
  Pallas kernels: 30 us -> 31.4 us
    pallas_call x1, Pallas kernels: 30 us -> 31.4 us  [per_device(): pl.pallas_call(functools.partial(kernel, n_gx, n_yz, chunk), out_shape=ja...]
where the time goes in v4:
time: 32.4 us; the launch traced here: 32.3 us
  Pallas kernels  31.4 us (97%)
  local copies, waits for them, and re-layouts  0.88 us (3%)
    pallas_call x1, Pallas kernels, per_device(): pl.pallas_call(functools.partial(kernel, n_gx, n_yz, chunk), out_shape=ja...  31.4 us
    unnamed x1, local copies, waits for them, and re-layouts  0.88 us

profile of v4, /device:TPU:0, one launch (start us, length us, event | category | flops | bytes accessed | tf_op | source)
XLA Modules:
  0.0 32.3 jit_solution(11344469421061060713)
XLA Ops:
  0.0 31.4 %shard_map.73 = f32[12,2,64,128]{3,2,1,0:T(8,128)S(1)} custom-call(f32[12,2,64,128]{3,2,1,0:T(8,128)} %res_hbm.1, f32[12,2,64,64]{3,2,1,0:T(8,128)} %inv_hbm.1, f32[8,64,64]{2,1,0:T(8,128)} %up_hbm.1, f32[8,64,64]{2,1,0:T(8,128)} %down_hbm.1, f32[8,64,64]{2,1,0:T(8,128)} %flux_hbm.1, s32[12,2,128]{2,1,0:T(2,128)} %cat_hbm.1, s32[2]{0:T(128)} %kinds_hbm.1), custom_call_target="tpu_custom_call" | custom-call | tf_op jit(solution)/shard_map/pallas_call | solution.py:488
  31.4 0.9 %copy.9 = f32[12,2,64,128]{3,2,1,0:T(8,128)} copy(f32[12,2,64,128]{3,2,1,0:T(8,128)S(1)} %shard_map.73) | data formatting | bytes 1572864

commit v5 on v4

--- a/solution.py
+++ b/solution.py
@@ -35,16 +35,27 @@
     return lax.fori_loop(0, count // unroll, several, carry)
 
 
+def cuts(cells):
+    small = cells // 6
+    if small == 0:
+        return ((0, cells),)
+    middle = (cells - 2 * small) // 2
+    bounds = (0, small, small + middle, cells - small, cells)
+    return tuple((a, b - a) for a, b in zip(bounds, bounds[1:]))
+
+
 def kernel(
-    n_gx, n_yz, chunk, res_hbm, inv_hbm, up_hbm, down_hbm, flux_hbm, cat_hbm, kinds_hbm, out,
+    n_gx, n_yz, res_hbm, inv_hbm, up_hbm, down_hbm, flux_hbm, cat_hbm, kinds_hbm, out,
     res, inv, up, down, flux, cat, kinds,
     snd, low, high, table, vt, ft, bt, hom, omega, path, echo, gain, fast, resp, cs, acc, gmap, given, taken,
     send_map, ahead, behind, mirror, side, wide_state, tall, into_state,
-    load_sem, halo_send, halo_recv, map_send, map_recv, vec_send, vec_recv,
+    load_sem, halo_send, halo_recv, map_send, map_recv, vec_send, vec_recv, ready,
 ):
     cells, groups, nv, nz = res.shape
     half = n_gx // 2
-    pieces = cells // chunk
+    parts = cuts(cells)
+    pieces = len(parts)
+    edge, chunk = parts[-1]
     gx = lax.axis_index("gx")
     yz = lax.axis_index("yz")
     partner = gx + 1 - 2 * lax.rem(gx, 2)
@@ -67,10 +78,18 @@
         return lax.rem(gx + 2 * k, n_gx)
 
     barrier = pltpu.get_barrier_semaphore()
-    for k in range(1, n_gx):
-        pl.semaphore_signal(
-            barrier, inc=1, device_id=(lax.rem(gx + k, n_gx), yz), device_id_type=MESH
-        )
+    bits = n_gx.bit_length() - 1
+    near = [
+        gx + (1 << k) * (1 - 2 * lax.rem(lax.div(gx, 1 << k), 2)) for k in range(bits)
+    ]
+
+    def hail(semaphore):
+        for device in near:
+            pl.semaphore_signal(
+                semaphore, inc=1, device_id=(device, yz), device_id_type=MESH
+            )
+
+    hail(barrier)
 
     @pl.when(has_low)
     def _():
@@ -80,10 +99,10 @@
     def _():
         pl.semaphore_signal(barrier, inc=1, device_id=(gx, yz + 1), device_id_type=MESH)
 
-    pl.semaphore_wait(barrier, n_gx - 1 + jnp.where(has_low, 1, 0) + jnp.where(has_high, 1, 0))
+    pl.semaphore_wait(barrier, bits + jnp.where(has_low, 1, 0) + jnp.where(has_high, 1, 0))
 
     def halo(direction, g, c):
-        part = pl.ds(c * chunk, chunk)
+        part = pl.ds(*parts[c])
         if direction == 0:
             src = snd.at[0, part] if g == 0 else res_hbm.at[part, 1]
             dst, where = low, yz + 1
@@ -99,33 +118,34 @@
             device_id_type=MESH,
         )
 
-    @pl.when(has_low)
-    def _():
-        for c in range(pieces):
-            halo(1, 0, c).start()
-
-    loads[0].wait()
-
-    for c in range(pieces):
-        for x in range(c * chunk, (c + 1) * chunk):
-            snd[0, x] = res[x, 0] - 8.0 * res[x, 1]
-
+    last = groups - 1
+
+    def emit(up, down):
         @pl.when(has_high)
         def _():
-            halo(0, 0, c).start()
-
-    @pl.when(has_high)
-    def _():
-        for c in range(pieces):
-            halo(0, 1, c).start()
-
-    for c in range(pieces):
-        for x in range(c * chunk, (c + 1) * chunk):
-            snd[1, x] = 8.0 * res[x, 0] - res[x, 1]
+            for g, c in up:
+                halo(0, g, c).start()
 
         @pl.when(has_low)
         def _():
-            halo(1, 1, c).start()
+            for g, c in down:
+                halo(1, g, c).start()
+
+    every = range(pieces)
+    emit([(last, 0)], [(0, c) for c in every])
+
+    loads[0].wait()
+
+    for c in every:
+        for x in range(parts[c][0], sum(parts[c])):
+            snd[0, x] = res[x, 0] - 8.0 * res[x, 1]
+        emit([(0, c)], [])
+
+    emit([(last, c) for c in every[1:]], [])
+    for c in every:
+        for x in range(parts[c][0], sum(parts[c])):
+            snd[1, x] = 8.0 * res[x, 0] - res[x, 1]
+        emit([], [(last, c)])
 
     @pl.when(jnp.logical_not(has_low))
     def _():
@@ -160,7 +180,9 @@
             put(bt, g, x, split(mul(v, held(g, 2))))
         return carry
 
+    hail(ready.at[0])
     loop(cells, steps, 0, 4)
+    pl.semaphore_wait(ready.at[0], bits)
 
     row = lax.broadcasted_iota(jnp.int32, (nv, 2 * nv), 0)
     col = lax.broadcasted_iota(jnp.int32, (nv, 2 * nv), 1)
@@ -230,6 +252,9 @@
             share(*where, peer(k), partner, half + k).wait_send()
 
     maps = (gmap, map_send, map_recv)
+    for r in range(1, bits - 1):
+        hail(ready.at[r])
+        pl.semaphore_wait(ready.at[r], bits)
     offer(*maps)
 
     for g in range(groups):
@@ -252,7 +277,6 @@
 
     loop(cells, hom_backward, 0)
 
-    edge = cells - chunk
     block = next(c for c in (12, 6, 4, 3, 2, 1) if cells % c == 0)
 
     def weight(g, x):
@@ -314,11 +338,12 @@
         for k in range(1, n_gx):
             parcel(g, lax.rem(gx + k, n_gx)).start()
 
-    def sweep_forward(g, first, count):
+    def sweep_forward(first, count):
         def forward(i, carry):
-            state = cs[g, i] + mul(get(ft, g, i), split(into_state[g]))
-            into_state[g] = state
-            cs[g, i] = state
+            for g in range(groups):
+                state = cs[g, i] + mul(get(ft, g, i), split(into_state[g]))
+                into_state[g] = state
+                cs[g, i] = state
             return carry
 
         lax.fori_loop(first, first + count, forward, 0)
@@ -376,25 +401,17 @@
     for g in range(groups):
         acc[g] = jnp.zeros((2 * nv, nz), F32)
 
-    for c in range(pieces):
-        arrive(0, c)
-    for x in range(0, cells, block):
-        local_forward(0, x, block, True)
-
-    last = groups - 1
     for n in range(chunk):
         x = edge + n
         fast[n, 0], fast[n, 1] = split(mul(get(gain, last, x), held(last, 0)))
         acc[last] += mul(get(gain, last, x), split(weight(last, x) * res[x, last]))
-    for g in range(groups):
-        into_state[g] = jnp.zeros((nv, nz), F32)
-    sweep_forward(0, 0, cells)
+
+    for c in every:
+        arrive(0, c)
+    for x in range(0, cells, block):
+        local_forward(0, x, block, True)
 
     relay(*maps)
-    first_wave = chunk if pieces > 1 else 0
-    if first_wave:
-        arrive(last, 0)
-        local_forward(last, 0, chunk, True)
     collect(*maps)
 
     for g in range(groups):
@@ -441,18 +458,24 @@
 
     dispatch(0)
 
-    for c in range(1, pieces - 1):
+    for c in every[:-1]:
         arrive(last, c)
-    for x in range(first_wave, edge, 6):
-        local_forward(last, x, min(6, edge - x), True)
+    for x in range(0, edge, 5):
+        local_forward(last, x, min(5, edge - x), True)
+    for g in range(groups):
+        into_state[g] = jnp.zeros((nv, nz), F32)
+
+    early = edge // 2
+    sweep_forward(0, early)
+
     arrive(last, pieces - 1)
     for n in range(chunk):
         x = edge + n
         acc[last] += mul((fast[n, 0], fast[n, 1]), split(weight(last, x) * slope(last, x)))
     dispatch(last)
     local_forward(last, edge, chunk, False)
-    for g in range(1, groups):
-        sweep_forward(g, 0, cells)
+
+    sweep_forward(early, cells - early)
     sweep_backward()
     for g in range(groups):
         turned(g)
@@ -479,14 +502,14 @@
 
 def per_device(n_gx, n_yz, residual, inverses, upwind, downwind, flux_y, kinds, volume_category):
     cells, groups, nv, nz = residual.shape
-    chunk = next(c for c in (3, 4, 2, 1) if cells % c == 0)
-    pieces = cells // chunk
+    pieces = len(cuts(cells))
+    chunk = cuts(cells)[-1][1]
     hbm = pl.BlockSpec(memory_space=pltpu.HBM)
     operands = (residual, inverses, upwind, downwind, flux_y, volume_category, kinds)
     square = pltpu.VMEM((groups, cells, 2, nv, nv), BF16)
     wide = pltpu.VMEM((groups, cells, nv, nz), F32)
     return pl.pallas_call(
-        functools.partial(kernel, n_gx, n_yz, chunk),
+        functools.partial(kernel, n_gx, n_yz),
         out_shape=jax.ShapeDtypeStruct(residual.shape, F32),
         in_specs=[hbm] * 7,
         out_specs=pl.BlockSpec(memory_space=pltpu.VMEM),
@@ -527,6 +550,7 @@
             pltpu.SemaphoreType.DMA((n_gx,)),
             pltpu.SemaphoreType.DMA((groups, n_gx)),
             pltpu.SemaphoreType.DMA((groups, n_gx)),
+            pltpu.SemaphoreType.REGULAR((max(n_gx.bit_length() - 2, 1),)),
         ],
         compiler_params=pltpu.CompilerParams(
             collective_id=0, has_side_effects=True, vmem_limit_bytes=48 * 1024 * 1024

time: 32.4 us -> 30.5 us (0.941)
  Pallas kernels: 31.4 us -> 29.5 us
    pallas_call x1, Pallas kernels: 31.4 us -> 29.5 us  [per_device(): pl.pallas_call(functools.partial(kernel, n_gx, n_yz), out_shape=jax.Shape...]
where the time goes in v5:
time: 30.5 us; the launch traced here: 30.4 us
  Pallas kernels  29.5 us (97%)
  local copies, waits for them, and re-layouts  0.88 us (3%)
    pallas_call x1, Pallas kernels, per_device(): pl.pallas_call(functools.partial(kernel, n_gx, n_yz), out_shape=jax.Shape...  29.5 us
    unnamed x1, local copies, waits for them, and re-layouts  0.88 us

profile of v5, /device:TPU:0, one launch (start us, length us, event | category | flops | bytes accessed | tf_op | source)
XLA Modules:
  0.0 30.4 jit_solution(12805531518788005219)
XLA Ops:
  0.0 29.5 %shard_map.73 = f32[12,2,64,128]{3,2,1,0:T(8,128)S(1)} custom-call(f32[12,2,64,128]{3,2,1,0:T(8,128)} %res_hbm.1, f32[12,2,64,64]{3,2,1,0:T(8,128)} %inv_hbm.1, f32[8,64,64]{2,1,0:T(8,128)} %up_hbm.1, f32[8,64,64]{2,1,0:T(8,128)} %down_hbm.1, f32[8,64,64]{2,1,0:T(8,128)} %flux_hbm.1, s32[12,2,128]{2,1,0:T(2,128)} %cat_hbm.1, s32[2]{0:T(128)} %kinds_hbm.1), custom_call_target="tpu_custom_call" | custom-call | tf_op jit(solution)/shard_map/pallas_call | solution.py:511
  29.5 0.9 %copy.9 = f32[12,2,64,128]{3,2,1,0:T(8,128)} copy(f32[12,2,64,128]{3,2,1,0:T(8,128)S(1)} %shard_map.73) | data formatting | bytes 1572864

commit v6 on v5

--- a/solution.py
+++ b/solution.py
@@ -406,12 +406,11 @@
         fast[n, 0], fast[n, 1] = split(mul(get(gain, last, x), held(last, 0)))
         acc[last] += mul(get(gain, last, x), split(weight(last, x) * res[x, last]))
 
+    relay(*maps)
     for c in every:
         arrive(0, c)
     for x in range(0, cells, block):
         local_forward(0, x, block, True)
-
-    relay(*maps)
     collect(*maps)
 
     for g in range(groups):
@@ -465,8 +464,8 @@
     for g in range(groups):
         into_state[g] = jnp.zeros((nv, nz), F32)
 
-    early = edge // 2
-    sweep_forward(0, early)
+    early = 0
+
 
     arrive(last, pieces - 1)
     for n in range(chunk):

time: 30.5 us -> 30.2 us (level)
  Pallas kernels: 29.5 us -> 29.1 us
    pallas_call x1, Pallas kernels: 29.5 us -> 29.1 us  [per_device(): pl.pallas_call(functools.partial(kernel, n_gx, n_yz), out_shape=jax.Shape...]
where the time goes in v6:
time: 30.2 us; the launch traced here: 30 us
  Pallas kernels  29.1 us (96%)
  local copies, waits for them, and re-layouts  0.88 us (3%)
    pallas_call x1, Pallas kernels, per_device(): pl.pallas_call(functools.partial(kernel, n_gx, n_yz), out_shape=jax.Shape...  29.1 us
    unnamed x1, local copies, waits for them, and re-layouts  0.88 us

profile of v6, /device:TPU:0, one launch (start us, length us, event | category | flops | bytes accessed | tf_op | source)
XLA Modules:
  0.0 30.0 jit_solution(9901415194887199084)
XLA Ops:
  0.0 29.1 %shard_map.73 = f32[12,2,64,128]{3,2,1,0:T(8,128)S(1)} custom-call(f32[12,2,64,128]{3,2,1,0:T(8,128)} %res_hbm.1, f32[12,2,64,64]{3,2,1,0:T(8,128)} %inv_hbm.1, f32[8,64,64]{2,1,0:T(8,128)} %up_hbm.1, f32[8,64,64]{2,1,0:T(8,128)} %down_hbm.1, f32[8,64,64]{2,1,0:T(8,128)} %flux_hbm.1, s32[12,2,128]{2,1,0:T(2,128)} %cat_hbm.1, s32[2]{0:T(128)} %kinds_hbm.1), custom_call_target="tpu_custom_call" | custom-call | tf_op jit(solution)/shard_map/pallas_call | solution.py:510
  29.1 0.9 %copy.9 = f32[12,2,64,128]{3,2,1,0:T(8,128)} copy(f32[12,2,64,128]{3,2,1,0:T(8,128)S(1)} %shard_map.73) | data formatting | bytes 1572864

commit v7 on v6

--- a/solution.py
+++ b/solution.py
@@ -47,7 +47,7 @@
 def kernel(
     n_gx, n_yz, res_hbm, inv_hbm, up_hbm, down_hbm, flux_hbm, cat_hbm, kinds_hbm, out,
     res, inv, up, down, flux, cat, kinds,
-    snd, low, high, table, vt, ft, bt, hom, omega, path, echo, gain, fast, resp, cs, acc, gmap, given, taken,
+    snd, low, high, table, vt, ft, bt, hom, omega, path, echo, gain, fast, zfast, resp, cs, acc, gmap, given, taken,
     send_map, ahead, behind, mirror, side, wide_state, tall, into_state,
     load_sem, halo_send, halo_recv, map_send, map_recv, vec_send, vec_recv, ready,
 ):
@@ -82,6 +82,11 @@
     near = [
         gx + (1 << k) * (1 - 2 * lax.rem(lax.div(gx, 1 << k), 2)) for k in range(bits)
     ]
+
+    def flip(k):
+        return gx + sum(near[b] - gx for b in range(bits) if k >> b & 1)
+
+    far_first = sorted(range(1, n_gx), key=lambda k: -bin(k >> 1).count("1"))
 
     def hail(semaphore):
         for device in near:
@@ -210,7 +215,7 @@
             path[g, 0], path[g, 1] = onward
         return carry
 
-    loop(cells, hom_forward, 0)
+    loop(cells, hom_forward, 0, 12)
     for g in range(groups):
         total = echo[g] + mul((path[g, 0], path[g, 1]), split(hom[g, cells]))
         gmap[gx, g * nv : (g + 1) * nv] = jnp.concatenate(
@@ -275,7 +280,7 @@
             tall[g] = mul(now, get(ft, g, x))
         return carry
 
-    loop(cells, hom_backward, 0)
+    loop(cells, hom_backward, 0, 4)
 
     block = next(c for c in (12, 6, 4, 3, 2, 1) if cells % c == 0)
 
@@ -329,12 +334,13 @@
             device_id_type=MESH,
         ).wait_recv()
 
+    def compose(g):
+        ah, al = split(acc[g])
+        for t in range(0, n_gx, 4):
+            z = tuple(send_map[g, m, t : t + 4].reshape(4 * nv, 2 * nv) for m in range(2))
+            given[g, t : t + 4] = mul(z, (ah, al)).reshape(4, nv, nz)
+
     def dispatch(g):
-        ah, al = split(acc[g])
-        for t in range(n_gx // 4):
-            zh = send_map[g, 0, 4 * t : 4 * t + 4].reshape(4 * nv, 2 * nv)
-            zl = send_map[g, 1, 4 * t : 4 * t + 4].reshape(4 * nv, 2 * nv)
-            given[g, 4 * t : 4 * t + 4] = mul((zh, zl), (ah, al)).reshape(4, nv, nz)
         for k in range(1, n_gx):
             parcel(g, lax.rem(gx + k, n_gx)).start()
 
@@ -346,7 +352,7 @@
                 cs[g, i] = state
             return carry
 
-        lax.fori_loop(first, first + count, forward, 0)
+        loop(count, lambda i, carry: forward(first + i, carry), 0, 4)
 
     def sweep_backward():
         for g in range(groups):
@@ -360,7 +366,7 @@
                 cs[g, x] = state
             return carry
 
-        lax.fori_loop(0, cells, backward, 0)
+        loop(cells, backward, 0, 4)
 
     def finish(g):
         head = jnp.zeros((nv, nz), F32)
@@ -403,7 +409,9 @@
 
     for n in range(chunk):
         x = edge + n
-        fast[n, 0], fast[n, 1] = split(mul(get(gain, last, x), held(last, 0)))
+        pair = split(mul(get(gain, last, x), held(last, 0)))
+        for m in range(2):
+            fast[m, :, n * nv : (n + 1) * nv] = pair[m]
         acc[last] += mul(get(gain, last, x), split(weight(last, x) * res[x, last]))
 
     relay(*maps)
@@ -411,6 +419,8 @@
         arrive(0, c)
     for x in range(0, cells, block):
         local_forward(0, x, block, True)
+    arrive(last, 0)
+    local_forward(last, 0, parts[0][1] if pieces > 1 else 0, True)
     collect(*maps)
 
     for g in range(groups):
@@ -435,7 +445,7 @@
             mirror[g, t + 1] = jnp.where(grow, step, unit)
         return carry
 
-    loop(n_gx - 2, chains, 0)
+    loop(n_gx - 2, chains, 0, 6)
 
     for g in range(groups):
         rows = slice(g * nv, (g + 1) * nv)
@@ -455,29 +465,42 @@
             send_map[g, 0, i], send_map[g, 1, i] = split(m)
         side[g] = sp
 
+    compose(0)
     dispatch(0)
 
-    for c in every[:-1]:
+    for t in range(0, n_gx, 4):
+        z = tuple(send_map[last, m, t : t + 4].reshape(4 * nv, 2 * nv) for m in range(2))
+        quick = split(mul(z, (fast[0], fast[1])))
+        for m in range(2):
+            zfast[m, t : t + 4] = quick[m].reshape(4, nv, chunk * nv)
+    for g in range(groups):
+        turned(g)
+    for g in range(groups):
+        into_state[g] = jnp.zeros((nv, nz), F32)
+
+    done = 0
+    for c in every[1:-1]:
         arrive(last, c)
-    for x in range(0, edge, 5):
-        local_forward(last, x, min(5, edge - x), True)
-    for g in range(groups):
-        into_state[g] = jnp.zeros((nv, nz), F32)
-
-    early = 0
-
+        local_forward(last, *parts[c], True)
+        if c < pieces - 2 and True:
+            sweep_forward(done, sum(parts[c]) - done)
+            done = sum(parts[c])
+    compose(last)
 
     arrive(last, pieces - 1)
-    for n in range(chunk):
-        x = edge + n
-        acc[last] += mul((fast[n, 0], fast[n, 1]), split(weight(last, x) * slope(last, x)))
+    late = split(
+        jnp.concatenate(
+            [weight(last, x) * slope(last, x) for x in range(edge, cells)], axis=0
+        )
+    )
+    for t in range(0, n_gx, 4):
+        z = tuple(zfast[m, t : t + 4].reshape(4 * nv, chunk * nv) for m in range(2))
+        given[last, t : t + 4] += mul(z, late).reshape(4, nv, nz)
     dispatch(last)
     local_forward(last, edge, chunk, False)
 
-    sweep_forward(early, cells - early)
+    sweep_forward(done, cells - done)
     sweep_backward()
-    for g in range(groups):
-        turned(g)
     for g in range(groups):
         finish(g)
 
@@ -527,7 +550,8 @@
             pltpu.VMEM((groups, 2, nv, nv), BF16),
             pltpu.VMEM((groups, nv, 2 * nv), F32),
             pltpu.VMEM((groups, cells, 2, 2 * nv, nv), BF16),
-            pltpu.VMEM((chunk, 2, 2 * nv, nv), BF16),
+            pltpu.VMEM((2, 2 * nv, chunk * nv), BF16),
+            pltpu.VMEM((2, n_gx, nv, chunk * nv), BF16),
             pltpu.VMEM((groups, 2, cells, nv, 2 * nv), BF16),
             wide,
             pltpu.VMEM((groups, 2 * nv, nz), F32),

time: 30.2 us -> 28.9 us (0.957)
  Pallas kernels: 29.1 us -> 27.9 us
    pallas_call x1, Pallas kernels: 29.1 us -> 27.9 us  [per_device(): pl.pallas_call(functools.partial(kernel, n_gx, n_yz), out_shape=jax.Shape...]
where the time goes in v7:
time: 28.9 us; the launch traced here: 28.8 us
  Pallas kernels  27.9 us (97%)
  local copies, waits for them, and re-layouts  0.88 us (3%)
    pallas_call x1, Pallas kernels, per_device(): pl.pallas_call(functools.partial(kernel, n_gx, n_yz), out_shape=jax.Shape...  27.9 us
    unnamed x1, local copies, waits for them, and re-layouts  0.88 us

profile of v7, /device:TPU:0, one launch (start us, length us, event | category | flops | bytes accessed | tf_op | source)
XLA Modules:
  0.0 28.8 jit_solution(4274328639214953440)
XLA Ops:
  0.0 27.9 %shard_map.73 = f32[12,2,64,128]{3,2,1,0:T(8,128)S(1)} custom-call(f32[12,2,64,128]{3,2,1,0:T(8,128)} %res_hbm.1, f32[12,2,64,64]{3,2,1,0:T(8,128)} %inv_hbm.1, f32[8,64,64]{2,1,0:T(8,128)} %up_hbm.1, f32[8,64,64]{2,1,0:T(8,128)} %down_hbm.1, f32[8,64,64]{2,1,0:T(8,128)} %flux_hbm.1, s32[12,2,128]{2,1,0:T(2,128)} %cat_hbm.1, s32[2]{0:T(128)} %kinds_hbm.1), custom_call_target="tpu_custom_call" | custom-call | tf_op jit(solution)/shard_map/pallas_call | solution.py:533
  27.9 0.9 %copy.9 = f32[12,2,64,128]{3,2,1,0:T(8,128)} copy(f32[12,2,64,128]{3,2,1,0:T(8,128)S(1)} %shard_map.73) | data formatting | bytes 1572864

commit v8 on v7

--- a/solution.py
+++ b/solution.py
@@ -188,6 +188,8 @@
     hail(ready.at[0])
     loop(cells, steps, 0, 4)
     pl.semaphore_wait(ready.at[0], bits)
+    if bits > 2:
+        hail(ready.at[1])
 
     row = lax.broadcasted_iota(jnp.int32, (nv, 2 * nv), 0)
     col = lax.broadcasted_iota(jnp.int32, (nv, 2 * nv), 1)
@@ -258,7 +260,8 @@
 
     maps = (gmap, map_send, map_recv)
     for r in range(1, bits - 1):
-        hail(ready.at[r])
+        if r > 1:
+            hail(ready.at[r])
         pl.semaphore_wait(ready.at[r], bits)
     offer(*maps)
 

time: 28.9 us -> 28.9 us (level)
  no operation moved by 1% of the time
where the time goes in v8:
time: 28.9 us; the launch traced here: 28.8 us
  Pallas kernels  27.9 us (97%)
  local copies, waits for them, and re-layouts  0.88 us (3%)
    pallas_call x1, Pallas kernels, per_device(): pl.pallas_call(functools.partial(kernel, n_gx, n_yz), out_shape=jax.Shape...  27.9 us
    unnamed x1, local copies, waits for them, and re-layouts  0.88 us

profile of v8, /device:TPU:0, one launch (start us, length us, event | category | flops | bytes accessed | tf_op | source)
XLA Modules:
  0.0 28.8 jit_solution(9191201133247256116)
XLA Ops:
  0.0 27.9 %shard_map.73 = f32[12,2,64,128]{3,2,1,0:T(8,128)S(1)} custom-call(f32[12,2,64,128]{3,2,1,0:T(8,128)} %res_hbm.1, f32[12,2,64,64]{3,2,1,0:T(8,128)} %inv_hbm.1, f32[8,64,64]{2,1,0:T(8,128)} %up_hbm.1, f32[8,64,64]{2,1,0:T(8,128)} %down_hbm.1, f32[8,64,64]{2,1,0:T(8,128)} %flux_hbm.1, s32[12,2,128]{2,1,0:T(2,128)} %cat_hbm.1, s32[2]{0:T(128)} %kinds_hbm.1), custom_call_target="tpu_custom_call" | custom-call | tf_op jit(solution)/shard_map/pallas_call | solution.py:536
  27.9 0.9 %copy.9 = f32[12,2,64,128]{3,2,1,0:T(8,128)} copy(f32[12,2,64,128]{3,2,1,0:T(8,128)S(1)} %shard_map.73) | data formatting | bytes 1572864

commit v9 on v8

--- a/solution.py
+++ b/solution.py
@@ -39,8 +39,8 @@
     small = cells // 6
     if small == 0:
         return ((0, cells),)
-    middle = (cells - 2 * small) // 2
-    bounds = (0, small, small + middle, cells - small, cells)
+    first = (small + 1) // 2
+    bounds = (0, first, cells // 2, cells - small, cells)
     return tuple((a, b - a) for a, b in zip(bounds, bounds[1:]))
 
 

time: 28.9 us -> 28.9 us (level)
  no operation moved by 1% of the time
where the time goes in v9:
time: 28.9 us; the launch traced here: 28.8 us
  Pallas kernels  27.9 us (97%)
  local copies, waits for them, and re-layouts  0.88 us (3%)
    pallas_call x1, Pallas kernels, per_device(): pl.pallas_call(functools.partial(kernel, n_gx, n_yz), out_shape=jax.Shape...  27.9 us
    unnamed x1, local copies, waits for them, and re-layouts  0.88 us

profile of v9, /device:TPU:0, one launch (start us, length us, event | category | flops | bytes accessed | tf_op | source)
XLA Modules:
  0.0 28.8 jit_solution(13035523673022647140)
XLA Ops:
  0.0 27.9 %shard_map.73 = f32[12,2,64,128]{3,2,1,0:T(8,128)S(1)} custom-call(f32[12,2,64,128]{3,2,1,0:T(8,128)} %res_hbm.1, f32[12,2,64,64]{3,2,1,0:T(8,128)} %inv_hbm.1, f32[8,64,64]{2,1,0:T(8,128)} %up_hbm.1, f32[8,64,64]{2,1,0:T(8,128)} %down_hbm.1, f32[8,64,64]{2,1,0:T(8,128)} %flux_hbm.1, s32[12,2,128]{2,1,0:T(2,128)} %cat_hbm.1, s32[2]{0:T(128)} %kinds_hbm.1), custom_call_target="tpu_custom_call" | custom-call | tf_op jit(solution)/shard_map/pallas_call | solution.py:536
  27.9 0.9 %copy.9 = f32[12,2,64,128]{3,2,1,0:T(8,128)} copy(f32[12,2,64,128]{3,2,1,0:T(8,128)S(1)} %shard_map.73) | data formatting | bytes 1572864
